TPU v7x, 32 devices: a whole 2x2x4 slice. The times are simulated.
32 devices in a mesh: grp: 2 (over x), tp: 8 (over z, y), rb: 2 (over core).
Axes of the slice: x: 2, y: 2, z: 4, core: 2. Of those that a mesh axis runs over, the one named last changes fastest.
Arguments:
- peram: bfloat16 [2048, 24, 2, 1024], P(('grp', 'tp'), None, None, 'rb'), parts along dimension 0, may hold values from -1 to 1
- src_elems: bfloat16 [14, 2, 256, 256], P('grp'), parts along dimension 0, may hold values from -0.25 to 0.25
- owner_times: int32 [16, 2], P('grp'), parts along dimension 0, may hold values from 0 to 23
- diag_mom: int32 [16, 2, 2], P(('grp', 'tp')), parts along dimension 0, may hold values from 0 to 6
- diag_count: int32 [16], P(('grp', 'tp')), parts along dimension 0, may hold values from 1 to 2, as said below
Outputs:
- corr: float32 [16, 2, 2, 2], P(('grp', 'tp')), parts along dimension 0
There are 2 independent parts, one for each index of `grp`. A program takes and returns all parts, laid end to end along the dimension named above; each array names one. Nothing has to cross between parts.
Inputs may be any that keep to these rules, and one draw needn't show every extreme that they name: `diag_count`: some pair has 2 assignments.
All inputs are finite; a program needn't handle non-finite values.
Results may differ from a plain program's by a relative error of at most 0.0031.
Values may be sent and summed in bfloat16 or wider, within the bound.
A program may use at most 128 MiB of HBM per device.

v0:
```python
import jax
import jax.numpy as jnp
from jax import lax
from jax.sharding import PartitionSpec as P


def paired_rhs(factor_part):
    swapped = jnp.stack([factor_part[:, 1], -factor_part[:, 0]], axis=1)
    return jnp.stack([factor_part, swapped], axis=0)


def contract_rows(left_rows, right_pair):
    return lax.dot_general(
        left_rows, right_pair, (((1, 2), (2, 3)), ((), ())), preferred_element_type=jnp.float32
    )


def trace_block(flipped, diag_block):
    block_f = diag_block.astype(jnp.float32)
    flip_f = flipped.astype(jnp.float32)
    real_sum = jnp.sum(flip_f[0] * block_f[:, 0] - flip_f[1] * block_f[:, 1])
    imag_sum = jnp.sum(flip_f[0] * block_f[:, 1] + flip_f[1] * block_f[:, 0])
    return (real_sum, imag_sum)


def shards(peram, src_elems, owner_times, diag_mom, diag_count):
    rb_count = lax.axis_size("rb")
    rb_rank = lax.axis_index("rb")
    picked = jnp.take(peram, owner_times, axis=1)
    arrived = lax.all_to_all(picked, "tp", split_axis=1, concat_axis=0, tiled=True)
    factor = arrived[:, 0]
    total_rows = factor.shape[0]
    row_count = total_rows // rb_count
    eig_count = src_elems.shape[-1]
    spin_total = total_rows // eig_count
    local_spins = row_count // eig_count
    diag_total = diag_mom.shape[1]
    right_pairs = [paired_rhs(factor[:, time_slot]) for time_slot in range(2)]
    summed = lax.psum_scatter(
        jnp.stack(
            [contract_rows(factor[:, time_slot], right_pairs[time_slot]) for time_slot in range(2)],
            axis=1,
        ),
        "rb",
        scatter_dimension=0,
        tiled=True,
    )
    meson_rows = summed.astype(jnp.bfloat16)
    meson_a = meson_rows[:, 0]
    meson_b = meson_rows[:, 1]
    owned = diag_count[0]
    results = []
    for slot_index in range(diag_total):
        elem_three = lax.dynamic_index_in_dim(
            src_elems, diag_mom[0, slot_index, 0], 0, keepdims=False
        )
        elem_four = lax.dynamic_index_in_dim(
            src_elems, diag_mom[0, slot_index, 1], 0, keepdims=False
        )
        flip_three = jnp.swapaxes(elem_three, 1, 2)
        flip_four = jnp.swapaxes(elem_four, 1, 2)
        right_four = jnp.stack(
            [
                jnp.stack([elem_four[0], elem_four[1]], axis=1),
                jnp.stack([-elem_four[1], elem_four[0]], axis=1),
            ],
            axis=0,
        )
        left_three = jnp.stack(
            [
                jnp.stack([flip_three[0], flip_three[1]], axis=-1),
                jnp.stack([flip_three[1], -flip_three[0]], axis=-1),
            ],
            axis=1,
        )
        mixed = jnp.concatenate(
            [
                lax.dot_general(
                    left_three,
                    meson_a[spin_local * eig_count : (spin_local + 1) * eig_count],
                    (((2, 3), (0, 1)), ((), ())),
                    preferred_element_type=jnp.float32,
                )
                for spin_local in range(local_spins)
            ],
            axis=0,
        )
        cross_re = jnp.zeros((), jnp.float32)
        cross_im = jnp.zeros((), jnp.float32)
        for spin_index in range(spin_total):
            col_block = meson_b[:, :, spin_index * eig_count : (spin_index + 1) * eig_count]
            product = lax.dot_general(
                col_block,
                right_four,
                (((1, 2), (0, 1)), ((), ())),
                preferred_element_type=jnp.float32,
            )
            partner = mixed[:, :, spin_index * eig_count : (spin_index + 1) * eig_count]
            cross_re = cross_re + jnp.sum(
                product[:, 0] * partner[:, 0] - product[:, 1] * partner[:, 1]
            )
            cross_im = cross_im + jnp.sum(
                product[:, 0] * partner[:, 1] + product[:, 1] * partner[:, 0]
            )
        three_re = jnp.zeros((), jnp.float32)
        three_im = jnp.zeros((), jnp.float32)
        four_re = jnp.zeros((), jnp.float32)
        four_im = jnp.zeros((), jnp.float32)
        for spin_local in range(local_spins):
            global_spin = rb_rank * local_spins + spin_local
            block_a = lax.dynamic_slice_in_dim(
                meson_a[spin_local * eig_count : (spin_local + 1) * eig_count],
                global_spin * eig_count,
                eig_count,
                2,
            )
            block_b = lax.dynamic_slice_in_dim(
                meson_b[spin_local * eig_count : (spin_local + 1) * eig_count],
                global_spin * eig_count,
                eig_count,
                2,
            )
            add_re, add_im = trace_block(flip_three, block_a)
            three_re = three_re + add_re
            three_im = three_im + add_im
            add_re, add_im = trace_block(flip_four, block_b)
            four_re = four_re + add_re
            four_im = four_im + add_im
        values = jnp.stack([cross_re, cross_im, three_re, three_im, four_re, four_im])
        values = lax.psum(values, "rb")
        results.append(values)
    stacked = jnp.stack(results)
    direct_re = stacked[:, 2] * stacked[:, 4] - stacked[:, 3] * stacked[:, 5]
    direct_im = stacked[:, 2] * stacked[:, 5] + stacked[:, 3] * stacked[:, 4]
    direct = jnp.stack([direct_re, direct_im], axis=-1)
    crossed = stacked[:, 0:2]
    values_all = 0.25 * jnp.stack([direct, crossed], axis=1)
    keep = (jnp.arange(diag_total, dtype=jnp.int32) < owned)[:, None, None]
    return jnp.where(keep, values_all, jnp.zeros_like(values_all))[None]


def solution(mesh):
    in_specs = (
        P(("grp", "tp"), None, None, "rb"),
        P("grp", None, None, None),
        P("grp", None),
        P(("grp", "tp"), None, None),
        P(("grp", "tp")),
    )
    out_specs = P(("grp", "tp"), None, None, None)
    return jax.shard_map(shards, mesh=mesh, in_specs=in_specs, out_specs=out_specs, check_vma=False)
```

profile of v0, /device:TPU:0, one launch (start us, length us, event | category | flops | bytes accessed | tf_op | source)
XLA Modules:
  0.0 233.8 jit_solution(16534536423233338884)
XLA Ops:
  8.1 13.4 %gather_fusion = bf16[16,128,2,512]{3,2,1,0:T(2,128)(2,1)} fusion(bf16[128,24,2,512]{3,2,1,0:T(2,128)(2,1)} %param.5, s32[1024]{0:T(1024)S(1)} %pad_clamp_fusion), kind=kCustom, calls=%fused_computation | custom fusion | bytes 8388672 | tf_op jit(solution)/shard_map/jit(_take)/gather | solution.py:29
  21.5 5.1 %copy.38 = bf16[16,128,2,512]{3,1,2,0:T(8,128)(2,1)} copy(bf16[16,128,2,512]{3,2,1,0:T(2,128)(2,1)} %gather_fusion) | data formatting | bytes 8388608 | tf_op jit(solution)/shard_map/jit(_take)/gather | solution.py:29
  26.7 2.6 %select_bitcast_fusion = bf16[128,8,2,2,512]{4,0,3,2,1:T(8,128)(2,1)S(1)} fusion(bf16[8,2,128,2,512]{4,2,3,1,0:T(8,128)(2,1)} %bitcast.384, pred[8,2]{1,0:T(8,128)(4,1)S(1)} %copy.36), kind=kLoop, calls=%fused_computation.38 | loop fusion | flops 2097152 | bytes 8388624 | tf_op jit(solution)/shard_map/jit(_take)/select_n | solution.py:29
  29.3 100.3 %all_to_all.15 = bf16[128,8,2,2,512]{4,0,3,2,1:T(8,128)(2,1)S(1)} all-to-all(bf16[128,8,2,2,512]{4,0,3,2,1:T(8,128)(2,1)S(1)} %select_bitcast_fusion), channel_id=1, replica_groups=mesh['grp'=2,'tp'=8,'rb'=2] {'tp'}, dimensions={1} | all-to-all | bytes 8388608 | tf_op jit(solution)/shard_map/all_to_all | solution.py:30
  130.1 0.7 slice_bitcast_fusion.3
  131.3 4.5 %fusion.8 = f32[1024,1,2,1024]{3,0,2,1:T(8,128)S(1)} fusion(bf16[1,1024,2,512]{3,1,2,0:T(8,128)(2,1)S(1)} %maximum_bitcast_fusion.1, bf16[1,1024,2,512]{3,1,2,0:T(8,128)(2,1)S(1)} %get-tuple-element.62, bf16[1024,2,2,512]{3,0,2,1:T(8,128)(2,1)S(1)} %bitcast.382), kind=kOutput, calls=%fused_computation.39 | convolution fusion | flops 4303355904 | bytes 14680064 | tf_op jit(solution)/shard_map/dot_general | solution.py:13
  136.0 4.5 %fusion.11 = f32[1024,1,2,1024]{3,0,2,1:T(8,128)S(1)} fusion(bf16[1,1024,2,512]{3,1,2,0:T(8,128)(2,1)S(1)} %maximum_bitcast_fusion, bf16[1,1024,2,512]{3,1,2,0:T(8,128)(2,1)S(1)} %get-tuple-element.61, bf16[1024,2,2,512]{3,0,2,1:T(8,128)(2,1)S(1)} %bitcast.383), kind=kOutput, calls=%fused_computation.40 | convolution fusion | flops 4303355904 | bytes 14680064 | tf_op jit(solution)/shard_map/dot_general | solution.py:13
  140.5 6.6 %pad_maximum_fusion = f32[1024,2,2,1024]{3,0,2,1:T(8,128)} fusion(f32[1024,1,2,1024]{3,0,2,1:T(8,128)S(1)} %fusion.8, f32[1024,1,2,1024]{3,0,2,1:T(8,128)S(1)} %fusion.11), kind=kLoop, calls=%fused_computation.1 | loop fusion | flops 4194304 | bytes 33554432 | tf_op jit(solution)/shard_map/stack | solution.py:40
  157.2 0.8 maximum_bitcast_fusion.6
  158.1 0.8 maximum_bitcast_fusion.2
  159.0 1.1 bitcast_convert_fusion.4
  160.1 0.9 convert_bitcast_fusion
  161.1 10.4 %reduce-scatter.2.cloned.1.call-done = f32[512,2,2,1024]{3,0,2,1:T(8,128)} async-done(((f32[1024,2,2,1024]{3,0,2,1:T(8,128)}), f32[512,2,2,1024]{3,0,2,1:T(8,128)}) %reduce-scatter.2.cloned.1.call-update) | async-done | bytes 8388624 | tf_op jit(solution)/shard_map/reduce_scatter | solution.py:39
  171.5 4.0 %convert_element_type.59 = bf16[512,2,2,1024]{3,0,2,1:T(8,128)(2,1)S(1)} convert(f32[512,2,2,1024]{3,0,2,1:T(8,128)} %reduce-scatter.2.cloned.1.call-done) | non-fusion elementwise | flops 2097152 | bytes 12582912 | tf_op jit(solution)/shard_map/convert_element_type | solution.py:48
  175.8 0.7 convolution_bitcast_fusion
  179.7 0.7 convolution_bitcast_fusion.2
  180.4 2.1 convolution_bitcast_fusion.3
  182.5 1.5 convolution_bitcast_fusion.9
  184.0 1.5 convolution_bitcast_fusion.10
  185.4 1.5 convolution_bitcast_fusion.8
  186.9 1.5 convolution_bitcast_fusion.11
  188.4 0.8 bitcast_convert_fusion.2
  189.2 0.8 bitcast_convert_fusion
  190.1 0.8 bitcast_convert_fusion.3
  190.9 0.9 bitcast_convert_fusion.1
  191.8 1.1 add_reduce_fusion.1
  192.9 1.1 add_reduce_fusion
  198.9 2.5 %add_reduce_fusion.14 = (f32[]{:T(128)}, f32[]{:T(128)}, f32[]{:T(128)}, f32[]{:T(128)}, f32[]{:T(128)}, /*index=5*/f32[]{:T(128)}, f32[]{:T(128)}, f32[]{:T(128)}) fusion(f32[2,256,256]{2,1,0:T(8,128)} %get-tuple-element.106, f32[256,2,256]{2,0,1:T(8,128)} %bitcast_convert_fusion.2, f32[2,256,256]{2,1,0:T(8,128)} %get-tuple-element.105, ...), kind=kLoop, calls=%fused_computation.152 | loop fusion | flops 2097144 | bytes 2097184 | tf_op jit(solution)/shard_map/reduce_sum | solution.py:22
  204.0 2.2 add_reduce_fusion.12
  208.8 3.5 %add_reduce_fusion.5 = (f32[]{:T(128)}, f32[]{:T(128)}, f32[]{:T(128)}, f32[]{:T(128)}, f32[512,1,256]{2,0,1:T(8,128)S(1)}) fusion(f32[512,2,256]{2,0,1:T(8,128)} %convolution_bitcast_fusion.9, f32[256,2,1024]{2,0,1:T(8,128)S(1)} %convolution_bitcast_fusion.2, f32[256,2,1024]{2,0,1:T(8,128)} %convolution_bitcast_fusion.3, ...), kind=kLoop, calls=%fused_computation.105 | loop fusion | flops 3276796 | bytes 6815760 | tf_op jit(solution)/shard_map/reduce_sum | solution.py:102
  212.3 1.3 add_reduce_fusion.4
  223.7 2.5 %all-reduce = (f32[1,6]{1,0:T(1,128)S(1)}, f32[1,6]{1,0:T(1,128)S(1)}) all-reduce(f32[1,6]{1,0:T(1,128)S(1)} %bitcast.390, f32[1,6]{1,0:T(1,128)S(1)} %bitcast.391), channel_id=1, replica_groups=mesh['grp'=2,'tp'=8,'rb'=2] {'rb'}, use_global_device_ids=true, to_apply=%region_34.35 | all-reduce | flops 12 | bytes 96 | tf_op jit(solution)/shard_map/psum | solution.py:130
  (62 shorter events, 9.2 us)
Async XLA Ops:
  6.5 165.0 %reduce-scatter.2.cloned.1.call-start = ((), (), s32[]{:S(2)}) async-start(), calls=%async_computation.2 | async-start | bytes 25165824 | tf_op jit(solution)/shard_map/reduce_scatter | solution.py:39
  147.1 0.7 copy-start.8
  147.1 8.7 %copy-start.4 = (bf16[7,2,256,256]{3,2,1,0:T(8,128)(2,1)S(1)}, bf16[7,2,256,256]{3,2,1,0:T(8,128)(2,1)}, u32[]{:S(2)}) copy-start(bf16[7,2,256,256]{3,2,1,0:T(8,128)(2,1)} %param.6) | copy-start | bytes 5505028
  175.7 1.5 copy-start.5
  179.7 2.8 %copy-start.6 = (bf16[1,256,2,256]{1,3,2,0:T(8,128)(2,1)S(1)}, bf16[1,256,2,256]{1,3,2,0:T(8,128)(2,1)}, u32[]{:S(2)}) copy-start(bf16[1,256,2,256]{1,3,2,0:T(8,128)(2,1)} %get-tuple-element.89) | copy-start | bytes 786436
  179.7 2.8 %copy-start.7 = (bf16[1,256,2,256]{1,3,2,0:T(8,128)(2,1)S(1)}, bf16[1,256,2,256]{1,3,2,0:T(8,128)(2,1)}, u32[]{:S(2)}) copy-start(bf16[1,256,2,256]{1,3,2,0:T(8,128)(2,1)} %get-tuple-element.90) | copy-start | bytes 786436
  192.9 11.1 %copy-start.1 = (f32[2,256,256]{2,1,0:T(8,128)S(1)}, f32[2,256,256]{2,1,0:T(8,128)}, u32[]{:S(2)}) copy-start(f32[2,256,256]{2,1,0:T(8,128)} %get-tuple-element.108) | copy-start | bytes 1572868
  206.2 6.1 %copy-start.2 = (f32[512,2,256]{2,0,1:T(8,128)S(1)}, f32[512,2,256]{2,0,1:T(8,128)}, u32[]{:S(2)}) copy-start(f32[512,2,256]{2,0,1:T(8,128)} %convolution_bitcast_fusion.8) | copy-start | bytes 3145732
  208.8 3.5 %copy-start = (f32[256,2,1024]{2,0,1:T(8,128)S(1)}, f32[256,2,1024]{2,0,1:T(8,128)}, u32[]{:S(2)}) copy-start(f32[256,2,1024]{2,0,1:T(8,128)} %convolution_bitcast_fusion.3) | copy-start | bytes 6291460
  208.8 3.5 %copy-start.3 = (f32[512,2,256]{2,0,1:T(8,128)S(1)}, f32[512,2,256]{2,0,1:T(8,128)}, u32[]{:S(2)}) copy-start(f32[512,2,256]{2,0,1:T(8,128)} %convolution_bitcast_fusion.11) | copy-start | bytes 3145732
Sparse Core Ops, SparseCore 0:
  147.3 24.2 reduce-scatter.1
where the time goes:
time: 235 us; the launch traced here: 234 us
  blocking collectives  103 us (44%)
  between operations  41.8 us (18%)
  other arithmetic  34.3 us (15%)
  local copies, waits for them, and re-layouts  23.4 us (10%)
  matrix products  21.1 us (9%)
  waiting for transfers between devices  10.5 us (4%)
    all_to_all x1, blocking collectives, shards(): lax.all_to_all(picked, 'tp', split_axis=1, concat_axis=0, tiled=True)  100 us
    gather x2, local copies, waits for them, and re-layouts, shards(): picked = jnp.take(peram, owner_times, axis=1)  18.5 us
    reduce_scatter x1, waiting for transfers between devices, shards(): lax.psum_scatter(jnp.stack([contract_rows(factor[:, time_slot], right_pai...  10.4 us
    dot_general x2, matrix products, contract_rows(): lax.dot_general(left_rows, right_pair, (((1, 2), (2, 3)), ((), ())), pref...  9.05 us
    dot_general x8, matrix products, shards(): lax.dot_general(col_block, right_four, (((1, 2), (0, 1)), ((), ())), pref...  7.78 us
    reduce_sum x4, other arithmetic, shards(): jnp.sum(product[:, 0] * partner[:, 1] + product[:, 1] * partner[:, 0])  7.01 us
    another operation x1, other arithmetic, shards(): jnp.stack([contract_rows(factor[:, time_slot], right_pairs[time_slot]) fo...  6.57 us
  transfers between devices with their start and end apart: 1, of which 1 were waited for; matrix products, arithmetic and copies ran while one was open for 2% of the time, Pallas kernels for 0%

commit v1 on v0

--- a/solution.py
+++ b/solution.py
@@ -27,7 +27,10 @@
     rb_count = lax.axis_size("rb")
     rb_rank = lax.axis_index("rb")
     picked = jnp.take(peram, owner_times, axis=1)
-    arrived = lax.all_to_all(picked, "tp", split_axis=1, concat_axis=0, tiled=True)
+    arrived = jnp.concatenate(
+        lax.all_to_all(jnp.stack(jnp.split(picked, lax.axis_size("tp"), axis=1)), "tp", 0, 0),
+        axis=0,
+    )
     factor = arrived[:, 0]
     total_rows = factor.shape[0]
     row_count = total_rows // rb_count

time: 235 us -> 244 us (1.038)
  matrix products: 21.1 us -> 27.7 us
    dot_general x8, matrix products: 7.78 us -> 11.8 us  [shards(): lax.dot_general(col_block, right_four, (((1, 2), (0, 1)), ((), ())), pref...]
    reduce_sum x4, other arithmetic: 7.01 us -> 10.3 us  [shards(): jnp.sum(product[:, 0] * partner[:, 1] + product[:, 1] * partner[:, 0])]
    dot_general x4, matrix products: 4.22 us -> 6.85 us  [shards(): lax.dot_general(left_three, meson_a[spin_local * eig_count:(spin_local +...]
where the time goes in v1:
time: 244 us; the launch traced here: 243 us
  blocking collectives  103 us (42%)
  between operations  42.5 us (17%)
  other arithmetic  34.7 us (14%)
  matrix products  27.7 us (11%)
  local copies, waits for them, and re-layouts  24.6 us (10%)
  waiting for transfers between devices  10.5 us (4%)
    all_to_all x1, blocking collectives, shards(): lax.all_to_all(jnp.stack(jnp.split(picked, lax.axis_size('tp'), axis=1)),...  100 us
    gather x2, local copies, waits for them, and re-layouts, shards(): picked = jnp.take(peram, owner_times, axis=1)  18.5 us
    dot_general x8, matrix products, shards(): lax.dot_general(col_block, right_four, (((1, 2), (0, 1)), ((), ())), pref...  11.8 us
    reduce_scatter x1, waiting for transfers between devices, shards(): lax.psum_scatter(jnp.stack([contract_rows(factor[:, time_slot], right_pai...  10.5 us
    reduce_sum x4, other arithmetic, shards(): jnp.sum(product[:, 0] * partner[:, 1] + product[:, 1] * partner[:, 0])  10.3 us
    dot_general x2, matrix products, contract_rows(): lax.dot_general(left_rows, right_pair, (((1, 2), (2, 3)), ((), ())), pref...  9.05 us
    dot_general x4, matrix products, shards(): lax.dot_general(left_three, meson_a[spin_local * eig_count:(spin_local +...  6.85 us
    another operation x1, other arithmetic, shards(): jnp.stack([contract_rows(factor[:, time_slot], right_pairs[time_slot]) fo...  6.57 us
  transfers between devices with their start and end apart: 1, of which 1 were waited for; matrix products, arithmetic and copies ran while one was open for 2% of the time, Pallas kernels for 0%

profile of v1, /device:TPU:0, one launch (start us, length us, event | category | flops | bytes accessed | tf_op | source)
XLA Modules:
  0.0 242.7 jit_solution(16414325433598682648)
XLA Ops:
  8.1 13.4 %gather_fusion = bf16[16,128,2,512]{3,2,1,0:T(2,128)(2,1)} fusion(bf16[128,24,2,512]{3,2,1,0:T(2,128)(2,1)} %param.5, s32[1024]{0:T(1024)S(1)} %pad_clamp_fusion), kind=kCustom, calls=%fused_computation | custom fusion | bytes 8388672 | tf_op jit(solution)/shard_map/jit(_take)/gather | solution.py:29
  21.5 5.1 %copy.54 = bf16[16,128,2,512]{3,1,2,0:T(8,128)(2,1)} copy(bf16[16,128,2,512]{3,2,1,0:T(2,128)(2,1)} %gather_fusion) | data formatting | bytes 8388608 | tf_op jit(solution)/shard_map/jit(_take)/gather | solution.py:29
  26.7 2.6 %select_bitcast_fusion = bf16[128,8,2,2,512]{4,0,3,2,1:T(8,128)(2,1)S(1)} fusion(bf16[8,2,128,2,512]{4,2,3,1,0:T(8,128)(2,1)} %bitcast.413, pred[8,2]{1,0:T(8,128)(4,1)S(1)} %copy.52), kind=kLoop, calls=%fused_computation.38 | loop fusion | flops 2097152 | bytes 8388624 | tf_op jit(solution)/shard_map/jit(_take)/select_n | solution.py:29
  29.7 100.3 %all_to_all.5 = bf16[8,128,1,2,2,512]{5,1,4,3,2,0:T(8,128)(2,1)S(1)} all-to-all(bf16[8,128,1,2,2,512]{5,1,4,3,2,0:T(8,128)(2,1)S(1)} %fusion.36), channel_id=1, replica_groups=mesh['grp'=2,'tp'=8,'rb'=2] {'tp'}, dimensions={0} | all-to-all | bytes 8388608 | tf_op jit(solution)/shard_map/all_to_all | solution.py:31
  131.6 4.5 %fusion.11 = f32[1024,1,2,1024]{3,0,2,1:T(8,128)S(1)} fusion(bf16[1,1024,2,512]{3,1,2,0:T(8,128)(2,1)S(1)} %maximum_bitcast_fusion, bf16[1,1024,2,512]{3,1,2,0:T(8,128)(2,1)S(1)} %get-tuple-element.61, bf16[1024,2,2,512]{3,0,2,1:T(8,128)(2,1)S(1)} %bitcast.411), kind=kOutput, calls=%fused_computation.40 | convolution fusion | flops 4303355904 | bytes 14680064 | tf_op jit(solution)/shard_map/dot_general | solution.py:13
  136.4 4.5 %fusion.8 = f32[1024,1,2,1024]{3,0,2,1:T(8,128)S(1)} fusion(bf16[1,1024,2,512]{3,1,2,0:T(8,128)(2,1)S(1)} %maximum_bitcast_fusion.1, bf16[1,1024,2,512]{3,1,2,0:T(8,128)(2,1)S(1)} %get-tuple-element.62, bf16[1024,2,2,512]{3,0,2,1:T(8,128)(2,1)S(1)} %bitcast.412), kind=kOutput, calls=%fused_computation.39 | convolution fusion | flops 4303355904 | bytes 14680064 | tf_op jit(solution)/shard_map/dot_general | solution.py:13
  140.9 6.6 %pad_maximum_fusion = f32[1024,2,2,1024]{3,0,2,1:T(8,128)} fusion(f32[1024,1,2,1024]{3,0,2,1:T(8,128)S(1)} %fusion.8, f32[1024,1,2,1024]{3,0,2,1:T(8,128)S(1)} %fusion.11), kind=kLoop, calls=%fused_computation.1 | loop fusion | flops 4194304 | bytes 33554432 | tf_op jit(solution)/shard_map/stack | solution.py:43
  158.4 0.8 maximum_bitcast_fusion.6
  159.4 1.1 convert_bitcast_fusion
  160.5 0.9 bitcast_convert_fusion.4
  161.4 10.5 %reduce-scatter.2.cloned.1.call-done = f32[512,2,2,1024]{3,0,2,1:T(8,128)} async-done(((f32[1024,2,2,1024]{3,0,2,1:T(8,128)}), f32[512,2,2,1024]{3,0,2,1:T(8,128)}) %reduce-scatter.2.cloned.1.call-update) | async-done | bytes 8388624 | tf_op jit(solution)/shard_map/reduce_scatter | solution.py:42
  171.9 4.0 %convert_element_type.59 = bf16[512,2,2,1024]{3,0,2,1:T(8,128)(2,1)S(1)} convert(f32[512,2,2,1024]{3,0,2,1:T(8,128)} %reduce-scatter.2.cloned.1.call-done) | non-fusion elementwise | flops 2097152 | bytes 12582912 | tf_op jit(solution)/shard_map/convert_element_type | solution.py:51
  177.3 1.4 convolution_bitcast_fusion.10
  178.8 1.5 convolution_bitcast_fusion.9
  180.2 2.0 convolution_bitcast_fusion.2
  182.3 2.0 convolution_bitcast_fusion.3
  184.3 1.5 convolution_bitcast_fusion.11
  185.8 1.5 convolution_bitcast_fusion.8
  187.3 1.5 convolution_bitcast_fusion.7
  188.7 1.5 convolution_bitcast_fusion.4
  190.2 1.5 convolution_bitcast_fusion.6
  192.5 2.1 convolution_bitcast_fusion
  194.6 1.4 convolution_bitcast_fusion.5
  196.1 0.9 bitcast_convert_fusion.2
  197.0 0.9 bitcast_convert_fusion.3
  197.8 1.1 add_reduce_fusion.12
  201.6 2.2 add_reduce_fusion.14
  206.3 4.3 %add_reduce_fusion.5 = (f32[]{:T(128)}, f32[]{:T(128)}, f32[]{:T(128)}, f32[]{:T(128)}, f32[512,1,256]{2,0,1:T(8,128)S(1)}) fusion(f32[512,2,256]{2,0,1:T(8,128)} %convolution_bitcast_fusion.9, f32[256,2,1024]{2,0,1:T(8,128)} %convolution_bitcast_fusion.2, f32[256,2,1024]{2,0,1:T(8,128)} %convolution_bitcast_fusion.3, ...), kind=kLoop, calls=%fused_computation.121 | loop fusion | flops 3276796 | bytes 6815760 | tf_op jit(solution)/shard_map/reduce_sum | solution.py:105
  210.8 1.2 add_reduce_fusion.4
  222.4 3.5 %add_reduce_fusion.1 = (f32[]{:T(128)}, f32[]{:T(128)}, f32[]{:T(128)}, f32[]{:T(128)}, f32[512,1,256]{2,0,1:T(8,128)S(1)}) fusion(f32[512,2,256]{2,0,1:T(8,128)} %convolution_bitcast_fusion.5, f32[256,2,1024]{2,0,1:T(8,128)} %convolution_bitcast_fusion, f32[256,2,1024]{2,0,1:T(8,128)S(1)} %convolution_bitcast_fusion.1, ...), kind=kLoop, calls=%fused_computation.113 | loop fusion | flops 3276796 | bytes 6815760 | tf_op jit(solution)/shard_map/reduce_sum | solution.py:105
  225.9 1.3 add_reduce_fusion
  232.6 2.5 %all-reduce = (f32[1,6]{1,0:T(1,128)S(1)}, f32[1,6]{1,0:T(1,128)S(1)}) all-reduce(f32[1,6]{1,0:T(1,128)S(1)} %bitcast.419, f32[1,6]{1,0:T(1,128)S(1)} %bitcast.418), channel_id=1, replica_groups=mesh['grp'=2,'tp'=8,'rb'=2] {'rb'}, use_global_device_ids=true, to_apply=%region_34.35 | all-reduce | flops 12 | bytes 96 | tf_op jit(solution)/shard_map/psum | solution.py:133
  (82 shorter events, 10.1 us)
Async XLA Ops:
  6.5 165.3 %reduce-scatter.2.cloned.1.call-start = ((), (), s32[]{:S(2)}) async-start(), calls=%async_computation.2 | async-start | bytes 25165824 | tf_op jit(solution)/shard_map/reduce_scatter | solution.py:42
  147.5 0.7 copy-start.14
  147.5 8.7 %copy-start.10 = (bf16[7,2,256,256]{3,2,1,0:T(8,128)(2,1)S(1)}, bf16[7,2,256,256]{3,2,1,0:T(8,128)(2,1)}, u32[]{:S(2)}) copy-start(bf16[7,2,256,256]{3,2,1,0:T(8,128)(2,1)} %param.6) | copy-start | bytes 5505028
  176.4 1.0 copy-start.11
  182.3 5.0 %copy-start.12 = (bf16[1,256,2,256]{1,3,2,0:T(8,128)(2,1)S(1)}, bf16[1,256,2,256]{1,3,2,0:T(8,128)(2,1)}, u32[]{:S(2)}) copy-start(bf16[1,256,2,256]{1,3,2,0:T(8,128)(2,1)} %get-tuple-element.93) | copy-start | bytes 786436
  182.3 5.0 %copy-start.13 = (bf16[1,256,2,256]{1,3,2,0:T(8,128)(2,1)S(1)}, bf16[1,256,2,256]{1,3,2,0:T(8,128)(2,1)}, u32[]{:S(2)}) copy-start(bf16[1,256,2,256]{1,3,2,0:T(8,128)(2,1)} %get-tuple-element.94) | copy-start | bytes 786436
  192.5 5.3 %copy-start.4 = (f32[2,256,256]{2,1,0:T(8,128)S(1)}, f32[2,256,256]{2,1,0:T(8,128)}, u32[]{:S(2)}) copy-start(f32[2,256,256]{2,1,0:T(8,128)} %get-tuple-element.107) | copy-start | bytes 1572868
  192.5 5.3 %copy-start.5 = (f32[2,256,256]{2,1,0:T(8,128)S(1)}, f32[2,256,256]{2,1,0:T(8,128)}, u32[]{:S(2)}) copy-start(f32[2,256,256]{2,1,0:T(8,128)} %get-tuple-element.108) | copy-start | bytes 1572868
  194.6 7.0 %copy-start.3 = (f32[2,256,256]{2,1,0:T(8,128)S(1)}, f32[2,256,256]{2,1,0:T(8,128)}, u32[]{:S(2)}) copy-start(f32[2,256,256]{2,1,0:T(8,128)} %get-tuple-element.106) | copy-start | bytes 1572868
  203.7 6.9 %copy-start.8 = (f32[512,2,256]{2,0,1:T(8,128)S(1)}, f32[512,2,256]{2,0,1:T(8,128)}, u32[]{:S(2)}) copy-start(f32[512,2,256]{2,0,1:T(8,128)} %convolution_bitcast_fusion.11) | copy-start | bytes 3145732
  206.3 4.3 %copy-start.1 = (f32[256,2,1024]{2,0,1:T(8,128)S(1)}, f32[256,2,1024]{2,0,1:T(8,128)}, u32[]{:S(2)}) copy-start(f32[256,2,1024]{2,0,1:T(8,128)} %convolution_bitcast_fusion.2) | copy-start | bytes 6291460
  206.3 4.3 %copy-start.2 = (f32[256,2,1024]{2,0,1:T(8,128)S(1)}, f32[256,2,1024]{2,0,1:T(8,128)}, u32[]{:S(2)}) copy-start(f32[256,2,1024]{2,0,1:T(8,128)} %convolution_bitcast_fusion.3) | copy-start | bytes 6291460
  206.3 4.5 %copy-start.9 = (f32[512,2,256]{2,0,1:T(8,128)S(1)}, f32[512,2,256]{2,0,1:T(8,128)}, u32[]{:S(2)}) copy-start(f32[512,2,256]{2,0,1:T(8,128)} %convolution_bitcast_fusion.8) | copy-start | bytes 3145732
  212.1 13.8 %copy-start.6 = (f32[512,2,256]{2,0,1:T(8,128)S(1)}, f32[512,2,256]{2,0,1:T(8,128)}, u32[]{:S(2)}) copy-start(f32[512,2,256]{2,0,1:T(8,128)} %convolution_bitcast_fusion.7) | copy-start | bytes 3145732
  222.4 3.5 %copy-start = (f32[256,2,1024]{2,0,1:T(8,128)S(1)}, f32[256,2,1024]{2,0,1:T(8,128)}, u32[]{:S(2)}) copy-start(f32[256,2,1024]{2,0,1:T(8,128)} %convolution_bitcast_fusion) | copy-start | bytes 6291460
  222.4 3.5 %copy-start.7 = (f32[512,2,256]{2,0,1:T(8,128)S(1)}, f32[512,2,256]{2,0,1:T(8,128)}, u32[]{:S(2)}) copy-start(f32[512,2,256]{2,0,1:T(8,128)} %convolution_bitcast_fusion.4) | copy-start | bytes 3145732
Sparse Core Ops, SparseCore 0:
  147.6 24.2 reduce-scatter.1
